TPU v7x, 256 devices: a whole 4x4x8 slice. The times are simulated.
256 devices in a mesh: rep: 2 (over core), req: 32 (over y, z), tp: 4 (over x).
Axes of the slice: x: 4, y: 4, z: 8, core: 2. Of those that a mesh axis runs over, the one named last changes fastest.
Arguments:
- hidden: bfloat16 [1024, 1536], P(('rep', 'req'), 'tp'), may hold values from -6 to 6
- lengths: int32 [2, 512], P(None, 'req'), may hold values from 16 to 1024, as said below
- migrate: int32 [32], P('req'), may hold values from 0 to 15
- kv_cache: bfloat16 [1024, 1024, 8, 128], P(('rep', 'req'), None, 'tp'), may hold values from -250 to 250
- attn_gain: float32 [1536], replicated, may hold values from 0.1 to 1.9
- moe_gain: float32 [1536], replicated, may hold values from 0.1 to 1.9
- w_query: bfloat16 [1536, 1536], P(None, 'tp'), may hold values from -0.15625 to 0.15625
- key_value_weight: bfloat16 [1536, 1024], P(None, 'tp'), may hold values from -0.15625 to 0.15625
- output_weight: bfloat16 [1536, 1536], P('tp'), may hold values from -0.25 to 0.25
- w_gateup: bfloat16 [64, 1536, 2, 512], P(('rep', 'req'), None, None, 'tp'), may hold values from -0.15625 to 0.15625
- w_down: bfloat16 [64, 512, 1536], P(('rep', 'req'), 'tp'), may hold values from -0.25 to 0.25
- expert_ids: int32 [1024, 8], P(('rep', 'req')), may hold values from 0 to 63, all different within a row; in each aligned block of 16 rows (0 to 15, 16 to 31, ...) at most 6 rows name the same one
- expert_gates: float32 [1024, 8], P(('rep', 'req')), may hold values from 0.1 to 0.4
Outputs:
- layer_out: bfloat16 [1024, 1536], P(('rep', 'req'), 'tp')
Inputs may be any that keep to these rules, and one draw needn't show every extreme that they name: A request attends to its first lengths positions and to its own new key. `expert_ids`: each row names 8 distinct experts; among the rows of one device (an aligned block of 16 rows) no expert is named more than 6 times, and in some blocks one expert is named exactly 6 times.
All inputs are finite; a program needn't handle non-finite values.
Results may differ from a plain program's by a relative error of at most 0.015.
Values may be sent and summed in bfloat16 or wider, within the bound.
A program may use at most 64 MiB of HBM per device.

v0:
```python
import jax
import jax.numpy as jnp
from jax import lax
from jax.sharding import PartitionSpec as P

HEAD_SIZE = 64
epsilon = 1e-06
rope_base = 10000.0
masked_score = -1e30


def swapped(value, axis, apart):
    return lax.ppermute(value, axis, [(i, i ^ 1 << apart) for i in range(lax.axis_size(axis))])


def rms_norm(values, gain):
    mean_square = jnp.mean(values * values, axis=-1, keepdims=True)
    return values * lax.rsqrt(mean_square + epsilon) * gain


def apply_rotation(values, position):
    half_width = values.shape[-1] // 2
    inv_freq = rope_base ** (-jnp.arange(half_width, dtype=jnp.float32) * 2.0 / values.shape[-1])
    angles = position.astype(jnp.float32)[:, None, None] * inv_freq
    cosine = jnp.cos(angles)
    sine_part = jnp.sin(angles)
    first_half = values[..., :half_width]
    second_half = values[..., half_width:]
    return jnp.concatenate(
        [
            first_half * cosine - second_half * sine_part,
            second_half * cosine + first_half * sine_part,
        ],
        axis=-1,
    )


def attention(
    token_part, kv_rows, request_extent, attn_gain, w_query, key_value_weight, output_weight
):
    tokens = lax.all_gather(token_part, "tp", axis=1, tiled=True)
    row_count = tokens.shape[0]
    head_dim = HEAD_SIZE
    local_kv = kv_rows.shape[2]
    local_query = w_query.shape[1] // head_dim
    group_size = local_query // local_kv
    normalized_input = rms_norm(tokens.astype(jnp.float32), attn_gain).astype(jnp.bfloat16)
    query_vectors = jnp.dot(normalized_input, w_query, preferred_element_type=jnp.float32).reshape(
        row_count, local_query, head_dim
    )
    key_value_rows = jnp.dot(
        normalized_input, key_value_weight, preferred_element_type=jnp.float32
    ).reshape(row_count, local_kv, 2 * head_dim)
    query_vectors = (
        apply_rotation(query_vectors, request_extent)
        .astype(jnp.bfloat16)
        .reshape(row_count, local_kv, group_size, head_dim)
    )
    key_new = apply_rotation(key_value_rows[..., :head_dim], request_extent).astype(jnp.bfloat16)
    value_new = key_value_rows[..., head_dim:].astype(jnp.bfloat16)
    score_scale = head_dim ** (-0.5)
    cache_keys = kv_rows[..., :head_dim]
    cache_values = kv_rows[..., head_dim:]
    scores = (
        jnp.einsum("rhgd,rthd->rhgt", query_vectors, cache_keys, preferred_element_type=jnp.float32)
        * score_scale
    )
    own_score = (
        jnp.einsum("rhgd,rhd->rhg", query_vectors, key_new, preferred_element_type=jnp.float32)
        * score_scale
    )
    positions = jnp.arange(kv_rows.shape[1], dtype=jnp.int32)
    visible = positions[None, None, None, :] < request_extent[:, None, None, None]
    scores = jnp.where(visible, scores, masked_score)
    row_peak = jnp.maximum(jnp.max(scores, axis=-1), own_score)
    cache_prob = jnp.exp(scores - row_peak[..., None])
    own_prob = jnp.exp(own_score - row_peak)
    denominator = jnp.sum(cache_prob, axis=-1) + own_prob
    cache_weight = (cache_prob / denominator[..., None]).astype(jnp.bfloat16)
    own_weight = (own_prob / denominator).astype(jnp.bfloat16)
    mixture = jnp.einsum(
        "rhgt,rthd->rhgd", cache_weight, cache_values, preferred_element_type=jnp.float32
    )
    mixture = (
        mixture
        + own_weight.astype(jnp.float32)[..., None] * value_new.astype(jnp.float32)[:, :, None, :]
    )
    context = mixture.reshape(row_count, local_query * head_dim).astype(jnp.bfloat16)
    partial_out = jnp.dot(context, output_weight, preferred_element_type=jnp.float32)
    return tokens.astype(jnp.float32) + lax.psum(partial_out.astype(jnp.bfloat16), "tp").astype(
        jnp.float32
    )


def shards(
    hidden,
    lengths,
    migrate,
    kv_cache,
    attn_gain,
    moe_gain,
    w_query,
    key_value_weight,
    output_weight,
    w_gateup,
    w_down,
    expert_ids,
    expert_gates,
):
    row_count = hidden.shape[0]
    replica = lax.axis_index("rep")
    slot_index = jnp.arange(row_count, dtype=jnp.int32)
    chosen_slot = migrate[0]
    is_moved = slot_index == chosen_slot
    own_span = lax.dynamic_index_in_dim(lengths, replica, 0, keepdims=False)
    other_span = lax.dynamic_index_in_dim(lengths, 1 - replica, 0, keepdims=False)
    picked_cache = lax.dynamic_slice_in_dim(kv_cache, chosen_slot, 1, 0)
    picked_row = lax.dynamic_slice_in_dim(hidden, chosen_slot, 1, 0)
    cache_width = picked_cache.size
    packed = jnp.concatenate([picked_cache.reshape(1, cache_width), picked_row], axis=1)
    arrived = swapped(packed, "rep", 0)
    moved_cache = arrived[:, :cache_width].reshape(picked_cache.shape)
    moved_row = arrived[:, cache_width:]
    served_cache = lax.dynamic_update_slice_in_dim(kv_cache, moved_cache, chosen_slot, 0)
    served_rows = lax.dynamic_update_slice_in_dim(hidden, moved_row, chosen_slot, 0)
    request_extent = jnp.where(is_moved, other_span, own_span)
    residual = attention(
        served_rows,
        served_cache,
        request_extent,
        attn_gain,
        w_query,
        key_value_weight,
        output_weight,
    )
    full_width = moe_gain.shape[0]
    quarter = full_width // lax.axis_size("tp")
    expert_in = rms_norm(residual, moe_gain).astype(jnp.bfloat16)
    own_residual = lax.dynamic_slice_in_dim(residual, lax.axis_index("tp") * quarter, quarter, 1)
    expert_count = lax.axis_size("rep") * lax.axis_size("req")
    top_count = expert_ids.shape[1]
    capacity = min(row_count, max(3, 3 * row_count * top_count // expert_count))
    flat_ids = expert_ids.reshape(-1)
    matches = (flat_ids[:, None] == jnp.arange(expert_count, dtype=jnp.int32)[None, :]).astype(
        jnp.int32
    )
    slot_rank = jnp.sum((jnp.cumsum(matches, axis=0) - matches) * matches, axis=1)
    slot_target = flat_ids * capacity + slot_rank
    slot_table = (
        slot_target[:, None] == jnp.arange(expert_count * capacity, dtype=jnp.int32)[None, :]
    ).astype(jnp.float32)
    route_table = slot_table.reshape(row_count, top_count, -1).sum(axis=1)
    gate_table = (
        (slot_table * expert_gates.reshape(-1, 1)).reshape(row_count, top_count, -1).sum(axis=1)
    )
    outbound = jnp.einsum(
        "rs,rd->sd", route_table.astype(jnp.bfloat16), expert_in, preferred_element_type=jnp.float32
    ).astype(jnp.bfloat16)
    outbound = outbound.reshape(expert_count, capacity, -1)
    gate_up = w_gateup[0].reshape(w_gateup.shape[1], -1)
    down_rows = w_down[0]
    arrived_rows = lax.all_to_all(outbound, ("rep", "req"), split_axis=0, concat_axis=0, tiled=True)
    model_width = arrived_rows.shape[2]
    flattened = arrived_rows.reshape(-1, model_width)
    projected = jnp.dot(flattened, gate_up, preferred_element_type=jnp.float32)
    split_at = projected.shape[1] // 2
    activation = (jax.nn.silu(projected[:, :split_at]) * projected[:, split_at:]).astype(
        jnp.bfloat16
    )
    expert_part = jnp.dot(activation, down_rows, preferred_element_type=jnp.float32)
    expert_part = expert_part.reshape(arrived_rows.shape[0], arrived_rows.shape[1], model_width)
    returned = lax.all_to_all(
        expert_part.astype(jnp.bfloat16), ("rep", "req"), split_axis=0, concat_axis=0, tiled=True
    ).astype(expert_part.dtype)
    returned_rows = returned.reshape(expert_count * capacity, -1)
    combined = jnp.dot(
        gate_table,
        returned_rows,
        precision=lax.Precision.HIGHEST,
        preferred_element_type=jnp.float32,
    )
    expert_mix = lax.psum_scatter(
        combined.astype(jnp.bfloat16), "tp", scatter_dimension=1, tiled=True
    ).astype(jnp.float32)
    return (own_residual + expert_mix).astype(jnp.bfloat16)


def solution(mesh):
    placed = (
        P(("rep", "req"), "tp"),
        P(None, "req"),
        P("req"),
        P(("rep", "req"), None, "tp", None),
        P(),
        P(),
        P(None, "tp"),
        P(None, "tp"),
        P("tp", None),
        P(("rep", "req"), None, None, "tp"),
        P(("rep", "req"), "tp", None),
        P(("rep", "req"), None),
        P(("rep", "req"), None),
    )
    return jax.shard_map(
        shards, mesh=mesh, in_specs=placed, out_specs=P(("rep", "req"), "tp"), check_vma=False
    )
```

profile of v0, /device:TPU:8, one launch (start us, length us, event | category | flops | bytes accessed | tf_op | source)
XLA Modules:
  0.0 226.3 jit_solution(14845780851035790938)
XLA Ops:
  6.5 0.8 copy.69
  8.0 1.4 constant_dynamic-slice_fusion.3
  9.6 4.4 %pad_maximum_fusion = bf16[1,262528]{1,0:T(2,128)(2,1)S(1)} fusion(bf16[1,384]{1,0:T(2,128)(2,1)S(1)} %constant_dynamic-slice_fusion.2, bf16[1,262144]{1,0:T(2,128)(2,1)S(1)} %reshape.200), kind=kLoop, calls=%fused_computation.12 | loop fusion | flops 1050112 | bytes 1050112 | tf_op jit(solution)/shard_map/concatenate | solution.py:120
  14.2 21.2 %copy.45 = bf16[16,1024,2,128]{1,3,2,0:T(8,128)(2,1)} copy(bf16[16,1024,2,128]{3,2,1,0:T(2,128)(2,1)} %param.16) | data formatting | bytes 16777216 | tf_op args[3]
  36.1 0.2 convert_reduce_fusion
  36.6 1.0 copy-done.2
  37.7 12.2 %all_gather.3 = bf16[16,1536]{1,0:T(8,128)(2,1)S(1)} all-gather(bf16[16,384]{1,0:T(8,128)(2,1)S(1)} %dynamic_update_slice.6), channel_id=1, replica_groups=mesh['rep'=2,'req'=32,'tp'=4] {'tp'}, dimensions={1}, use_global_device_ids=true | all-gather | bytes 61440 | tf_op jit(solution)/shard_map/all_gather | solution.py:41
  49.9 9.9 %slice_reduce_fusion = bf16[262144]{0:T(1024)(128)(2,1)S(1)} fusion(bf16[1,262528]{1,0:T(2,128)(2,1)} %copy-done.2), kind=kLoop, calls=%fused_computation.13 | loop fusion | bytes 1048576 | tf_op jit(solution)/shard_map/slice | solution.py:122
  59.8 0.4 copy.46
  60.4 0.3 fusion.36
  60.8 1.4 fusion.34
  62.5 0.9 constant_dynamic-update-slice_fusion
  63.5 0.2 fusion.31
  63.7 3.0 %fusion.44 = (f32[16,2,3]{2,1,0:T(2,128)S(1)}, f32[16,2,3,1024]{3,2,1,0:T(4,128)S(1)}) fusion(bf16[16,1024,2,128]{1,3,2,0:T(8,128)(2,1)} %constant_dynamic-update-slice_fusion, bf16[16,2,3,32]{3,2,1,0:T(4,128)(2,1)S(1)} %copy.44, bf16[16,2,3,32]{3,2,1,0:T(4,128)(2,1)S(1)} %copy.43, pred[16,1024]{1,0:T(8,128)(4,1)S(1)} %iota_compare_fusion.2), kind=kOutput, calls=%fused_computation.77 | convolution fusion | flops 12902304 | bytes 4616576 | tf_op jit(solution)/shard_map/rhgd,rthd->rhgt/dot_general | solution.py:65
  66.8 0.3 fusion.19
  67.2 3.5 %fusion.13 = bf16[16,2,3,64]{3,2,1,0:T(4,128)(2,1)S(1)} fusion(bf16[16,1024,2,128]{1,3,2,0:T(8,128)(2,1)} %constant_dynamic-update-slice_fusion, f32[16,2,3,1024]{3,2,1,0:T(4,128)S(1)} %get-tuple-element.20, f32[16,2,3]{2,1,0:T(2,128)S(1)} %get-tuple-element.14, f32[16,2,3]{2,1,0:T(2,128)S(1)} %multiply_maximum_fusion, f32[16,2,64]{2,1,0:T(2,128)S(1)} %fusion.38, ...), kind=kOutput, calls=%fused_computation.11 | convolution fusion | flops 12896256 | bytes 4609152 | tf_op jit(solution)/shard_map/rhgt,rthd->rhgd/dot_general | solution.py:81
  70.7 0.3 convolution_convert_fusion.3
  71.0 17.0 %psum.7 = bf16[16,1536]{1,0:T(8,128)(2,1)S(1)} all-reduce(bf16[16,1536]{1,0:T(8,128)(2,1)S(1)} %convolution_convert_fusion.3), channel_id=1, replica_groups=mesh['rep'=2,'req'=32,'tp'=4] {'tp'}, use_global_device_ids=true, to_apply=%region_3.4 | all-reduce | flops 24576 | bytes 98304 | tf_op jit(solution)/shard_map/psum | solution.py:90
  88.2 1.5 convolution_convert_fusion
  89.7 2.2 reshape.204
  91.9 51.9 %all_to_all.10 = bf16[64,6,1536]{2,1,0:T(8,128)(2,1)} all-to-all(bf16[64,6,1536]{2,1,0:T(8,128)(2,1)S(1)} %reshape.204), channel_id=1, replica_groups=mesh['rep'=2,'req'=32,'tp'=4] {'rep','req'}, dimensions={0} | all-to-all | bytes 2359296 | tf_op jit(solution)/shard_map/all_to_all | solution.py:162
  143.8 2.3 %reshape.205 = bf16[384,1536]{1,0:T(8,128)(2,1)S(1)} reshape(bf16[64,6,1536]{2,1,0:T(8,128)(2,1)} %all_to_all.10) | data formatting | bytes 2359296 | tf_op jit(solution)/shard_map/reshape | solution.py:164
  146.1 1.7 fusion.16
  147.9 0.4 convolution_convert_fusion.1
  148.4 0.7 copy.51
  149.0 45.9 %all_to_all.11 = bf16[64,6,1536]{2,1,0:T(8,128)(2,1)S(1)} all-to-all(bf16[64,6,1536]{2,1,0:T(8,128)(2,1)S(1)} %copy.51), channel_id=1, replica_groups=mesh['rep'=2,'req'=32,'tp'=4] {'rep','req'}, dimensions={0} | all-to-all | bytes 2359296 | tf_op jit(solution)/shard_map/all_to_all | solution.py:172
  195.0 1.2 reshape.206
  196.2 1.8 convolution_convert_fusion.2
  198.0 0.9 copy.54
  199.0 18.9 %reduce-scatter.4.cloned.1.call-done = bf16[384,16]{1,0:T(8,128)(2,1)} async-done(((bf16[1536,16]{1,0:T(8,128)(2,1)}), bf16[384,16]{1,0:T(8,128)(2,1)}) %reduce-scatter.4.cloned.1.call-update) | async-done | bytes 12304
  217.9 1.0 copy.55
  218.9 0.6 add_convert_fusion.1
  (56 shorter events, 2.4 us)
Async XLA Ops:
  6.5 64.2 %copy-start = (bf16[384,1536]{1,0:T(8,128)(2,1)S(1)}, bf16[384,1536]{1,0:T(8,128)(2,1)}, u32[]{:S(2)}) copy-start(bf16[384,1536]{1,0:T(8,128)(2,1)} %param.21) | copy-start | bytes 3538948
  6.5 211.4 %reduce-scatter.4.cloned.1.call-start = ((), (), s32[]{:S(2)}) async-start(), calls=%async_computation.3 | async-start | bytes 491520
  14.0 21.3 %copy-start.6 = (s32[16,8]{0,1:T(8,128)S(1)}, s32[16,8]{0,1:T(8,128)}, u32[]{:S(2)}) copy-start(s32[16,8]{0,1:T(8,128)} %param.24) | copy-start | bytes 1540
  14.1 22.0 %copy-start.7 = (f32[16,8]{0,1:T(8,128)S(1)}, f32[16,8]{0,1:T(8,128)}, u32[]{:S(2)}) copy-start(f32[16,8]{0,1:T(8,128)} %param.25) | copy-start | bytes 1540
  14.1 22.3 %copy-start.8 = (s32[2,16]{1,0:T(2,128)S(1)}, s32[2,16]{1,0:T(2,128)}, u32[]{:S(2)}) copy-start(s32[2,16]{1,0:T(2,128)} %param.14) | copy-start | bytes 388
  14.1 22.5 %collective-permute-start = (bf16[1,262528]{1,0:T(2,128)(2,1)S(1)}, bf16[1,262528]{1,0:T(2,128)(2,1)S(1)}, u32[]{:S(2)}, u32[]{:S(2)}) collective-permute-start(bf16[1,262528]{1,0:T(2,128)(2,1)S(1)} %pad_maximum_fusion), channel_id=1, source_target_pairs={{0,128},{128,0},{1,129},{129,1},{2,130},{130,2},{3,131},{131,3},{4... | collective-permute-start | bytes 1575176 | tf_op jit(solution)/shard_map/ppermute | solution.py:13
  36.6 1.1 copy-start.2
  49.9 10.4 %copy-start.1 = (bf16[1536,384]{1,0:T(8,128)(2,1)S(1)}, bf16[1536,384]{1,0:T(8,128)(2,1)}, u32[]{:S(2)}) copy-start(bf16[1536,384]{1,0:T(8,128)(2,1)} %param.19) | copy-start | bytes 3538948
  49.9 10.4 %copy-start.4 = (f32[1536]{0:T(1024)S(1)}, f32[1536]{0:T(1024)}, u32[]{:S(2)}) copy-start(f32[1536]{0:T(1024)} %param.17) | copy-start | bytes 18436
  70.6 17.6 %copy-start.5 = (f32[1536]{0:T(1024)S(1)}, f32[1536]{0:T(1024)}, u32[]{:S(2)}) copy-start(f32[1536]{0:T(1024)} %param.18) | copy-start | bytes 18436
  146.1 1.8 copy-start.3
Sparse Core Ops, SparseCore 0:
  199.1 18.7 reduce-scatter.3
where the time goes:
time: 227 us; the launch traced here: 226 us
  blocking collectives  127 us (56%)
  local copies, waits for them, and re-layouts  44.7 us (20%)
  waiting for transfers between devices  18.9 us (8%)
  between operations  14.4 us (6%)
  matrix products  14.1 us (6%)
  other arithmetic  6.97 us (3%)
    all_to_all x1, blocking collectives, shards(): lax.all_to_all(outbound, ('rep', 'req'), split_axis=0, concat_axis=0, til...  51.9 us
    all_to_all x1, blocking collectives, shards(): lax.all_to_all(expert_part.astype(jnp.bfloat16), ('rep', 'req'), split_ax...  45.9 us
    unnamed x24, local copies, waits for them, and re-layouts  25.1 us
    unnamed x2, waiting for transfers between devices  18.9 us
    psum x1, blocking collectives, attention(): lax.psum(partial_out.astype(jnp.bfloat16), 'tp').astype(jnp.float32)  17 us
    all_gather x1, blocking collectives, attention(): tokens = lax.all_gather(token_part, 'tp', axis=1, tiled=True)  12.2 us
    slice x1, local copies, waits for them, and re-layouts, shards(): moved_cache = arrived[:, :cache_width].reshape(picked_cache.shape)  9.86 us
  transfers between devices with their start and end apart: 2, of which 1 were waited for; matrix products, arithmetic and copies ran while one was open for 10% of the time, Pallas kernels for 0%

commit v1 on v0

--- a/solution.py
+++ b/solution.py
@@ -7,6 +7,24 @@
 epsilon = 1e-06
 rope_base = 10000.0
 masked_score = -1e30
+
+
+def ring_gather(shard, axis, dim):
+    ways, here, step = (lax.axis_size(axis), lax.axis_index(axis), shard.shape[dim])
+    shape = [n * ways if d == dim else n for d, n in enumerate(shard.shape)]
+    full = lax.dynamic_update_slice_in_dim(
+        jnp.zeros(shape, shard.dtype), shard, here * step, axis=dim
+    )
+    going_up = going_down = shard
+    for far in range(1, ways // 2 + 1):
+        going_up = lax.ppermute(going_up, axis, [(d, (d + 1) % ways) for d in range(ways)])
+        full = lax.dynamic_update_slice_in_dim(full, going_up, (here - far) % ways * step, axis=dim)
+        if 2 * far < ways:
+            going_down = lax.ppermute(going_down, axis, [(d, (d - 1) % ways) for d in range(ways)])
+            full = lax.dynamic_update_slice_in_dim(
+                full, going_down, (here + far) % ways * step, axis=dim
+            )
+    return full
 
 
 def swapped(value, axis, apart):
@@ -38,7 +56,7 @@
 def attention(
     token_part, kv_rows, request_extent, attn_gain, w_query, key_value_weight, output_weight
 ):
-    tokens = lax.all_gather(token_part, "tp", axis=1, tiled=True)
+    tokens = ring_gather(token_part, "tp", 1)
     row_count = tokens.shape[0]
     head_dim = HEAD_SIZE
     local_kv = kv_rows.shape[2]

time: 227 us -> 219 us (0.965)
  blocking collectives: 127 us -> 113 us
  waiting for transfers between devices: 18.9 us -> 23.8 us
  starting transfers between devices: 0.09 us -> 3.86 us
    all_gather x1 -> x0, blocking collectives: 12.2 us -> none  [attention(): tokens = lax.all_gather(token_part, 'tp', axis=1, tiled=True)]
    ppermute x0 -> x3, waiting for transfers between devices: none -> 4.61 us  [the longest x2 4.61 us: ring_gather(): lax.ppermute(going_up, axis, [(d, (d + 1) % ways) for d in range(ways)])]
    ppermute x0 -> x3, starting transfers between devices: none -> 3.85 us  [the longest x2 2.11 us: ring_gather(): lax.ppermute(going_up, axis, [(d, (d + 1) % ways) for d in range(ways)])]
  transfers between devices with their start and end apart: 2 -> 5, of which waited for: 1 -> 2; matrix products, arithmetic and copies ran while one was open for 10% -> 15% of each run, Pallas kernels for 0% -> 0%
where the time goes in v1:
time: 219 us; the launch traced here: 218 us
  blocking collectives  113 us (52%)
  local copies, waits for them, and re-layouts  42.6 us (19%)
  waiting for transfers between devices  23.8 us (11%)
  between operations  14.4 us (7%)
  matrix products  13 us (6%)
  other arithmetic  7.74 us (4%)
  starting transfers between devices  3.86 us (2%)
    all_to_all x1, blocking collectives, shards(): lax.all_to_all(outbound, ('rep', 'req'), split_axis=0, concat_axis=0, til...  51.9 us
    all_to_all x1, blocking collectives, shards(): lax.all_to_all(expert_part.astype(jnp.bfloat16), ('rep', 'req'), split_ax...  45.9 us
    unnamed x24, local copies, waits for them, and re-layouts  24.1 us
    unnamed x2, waiting for transfers between devices  19.2 us
    psum x1, blocking collectives, attention(): lax.psum(partial_out.astype(jnp.bfloat16), 'tp').astype(jnp.float32)  15 us
    slice x1, local copies, waits for them, and re-layouts, shards(): moved_cache = arrived[:, :cache_width].reshape(picked_cache.shape)  8.75 us
    concatenate x1, other arithmetic, shards(): jnp.concatenate([picked_cache.reshape(1, cache_width), picked_row], axis=1)  5.18 us
    ppermute x2, waiting for transfers between devices, ring_gather(): lax.ppermute(going_up, axis, [(d, (d + 1) % ways) for d in range(ways)])  4.61 us
  transfers between devices with their start and end apart: 5, of which 2 were waited for; matrix products, arithmetic and copies ran while one was open for 15% of the time, Pallas kernels for 0%

profile of v1, /device:TPU:8, one launch (start us, length us, event | category | flops | bytes accessed | tf_op | source)
XLA Modules:
  0.0 218.2 jit_solution(18003673097740814038)
XLA Ops:
  6.5 0.8 copy.73
  8.0 1.4 constant_dynamic-slice_fusion.3
  9.6 5.2 %pad_maximum_fusion = bf16[1,262528]{1,0:T(2,128)(2,1)} fusion(bf16[1,384]{1,0:T(2,128)(2,1)S(1)} %constant_dynamic-slice_fusion.2, bf16[1,262144]{1,0:T(2,128)(2,1)S(1)} %reshape.200), kind=kLoop, calls=%fused_computation.12 | loop fusion | flops 1050112 | bytes 1050112 | tf_op jit(solution)/shard_map/concatenate | solution.py:138
  14.8 21.2 %copy.45 = bf16[16,1024,2,128]{1,3,2,0:T(8,128)(2,1)} copy(bf16[16,1024,2,128]{3,2,1,0:T(2,128)(2,1)} %param.16) | data formatting | bytes 16777216 | tf_op args[3]
  37.3 1.6 collective-permute-start.1
  38.9 1.7 collective-permute-start.2
  40.6 8.8 %slice_reduce_fusion = bf16[262144]{0:T(1024)(128)(2,1)S(1)} fusion(bf16[1,262528]{1,0:T(2,128)(2,1)S(1)} %collective-permute-done), kind=kLoop, calls=%fused_computation.13 | loop fusion | bytes 1048576 | tf_op jit(solution)/shard_map/slice | solution.py:140
  49.4 0.4 copy.46
  49.9 0.9 constant_dynamic-update-slice_fusion
  50.8 0.5 collective-permute-start.3
  51.3 4.6 %collective-permute-done.3 = bf16[16,384]{1,0:T(8,128)(2,1)S(1)} collective-permute-done((bf16[16,384]{1,0:T(8,128)(2,1)S(1)}, bf16[16,384]{1,0:T(8,128)(2,1)S(1)}, u32[]{:S(2)}, u32[]{:S(2)}) %collective-permute-start.3) | collective-permute-done | bytes 12320 | tf_op jit(solution)/shard_map/ppermute | solution.py:20
  56.1 0.3 fusion.36
  56.5 0.3 fusion.34
  57.4 3.0 %fusion.44 = (f32[16,2,3]{2,1,0:T(2,128)S(1)}, f32[16,2,3,1024]{3,2,1,0:T(4,128)S(1)}) fusion(bf16[16,1024,2,128]{1,3,2,0:T(8,128)(2,1)} %constant_dynamic-update-slice_fusion, bf16[16,2,3,32]{3,2,1,0:T(4,128)(2,1)S(1)} %copy.44, bf16[16,2,3,32]{3,2,1,0:T(4,128)(2,1)S(1)} %copy.43, pred[16,1024]{1,0:T(8,128)(4,1)S(1)} %iota_compare_fusion.2), kind=kOutput, calls=%fused_computation.81 | convolution fusion | flops 12902304 | bytes 4616576 | tf_op jit(solution)/shard_map/rhgd,rthd->rhgt/dot_general | solution.py:83
  60.5 0.3 fusion.19
  60.9 3.5 %fusion.13 = bf16[16,2,3,64]{3,2,1,0:T(4,128)(2,1)S(1)} fusion(bf16[16,1024,2,128]{1,3,2,0:T(8,128)(2,1)} %constant_dynamic-update-slice_fusion, f32[16,2,3,1024]{3,2,1,0:T(4,128)S(1)} %get-tuple-element.20, f32[16,2,3]{2,1,0:T(2,128)S(1)} %get-tuple-element.14, f32[16,2,3]{2,1,0:T(2,128)S(1)} %multiply_maximum_fusion, f32[16,2,64]{2,1,0:T(2,128)S(1)} %fusion.38, ...), kind=kOutput, calls=%fused_computation.11 | convolution fusion | flops 12896256 | bytes 4609152 | tf_op jit(solution)/shard_map/rhgt,rthd->rhgd/dot_general | solution.py:99
  64.4 0.3 convolution_convert_fusion.3
  64.7 15.0 %psum.7 = bf16[16,1536]{1,0:T(8,128)(2,1)S(1)} all-reduce(bf16[16,1536]{1,0:T(8,128)(2,1)S(1)} %convolution_convert_fusion.3), channel_id=1, replica_groups=mesh['rep'=2,'req'=32,'tp'=4] {'tp'}, use_global_device_ids=true, to_apply=%region_3.4 | all-reduce | flops 24576 | bytes 98304 | tf_op jit(solution)/shard_map/psum | solution.py:108
  79.8 1.5 convolution_convert_fusion
  81.3 2.2 %reshape.204 = bf16[64,6,1536]{2,1,0:T(8,128)(2,1)S(1)} reshape(bf16[384,1536]{1,0:T(8,128)(2,1)} %convolution_convert_fusion) | data formatting | bytes 2359296 | tf_op jit(solution)/shard_map/reshape | solution.py:177
  83.6 51.9 %all_to_all.10 = bf16[64,6,1536]{2,1,0:T(8,128)(2,1)} all-to-all(bf16[64,6,1536]{2,1,0:T(8,128)(2,1)S(1)} %reshape.204), channel_id=1, replica_groups=mesh['rep'=2,'req'=32,'tp'=4] {'rep','req'}, dimensions={0} | all-to-all | bytes 2359296 | tf_op jit(solution)/shard_map/all_to_all | solution.py:180
  135.4 2.3 %reshape.205 = bf16[384,1536]{1,0:T(8,128)(2,1)S(1)} reshape(bf16[64,6,1536]{2,1,0:T(8,128)(2,1)} %all_to_all.10) | data formatting | bytes 2359296 | tf_op jit(solution)/shard_map/reshape | solution.py:182
  137.7 1.7 fusion.16
  139.5 0.4 convolution_convert_fusion.1
  140.0 0.7 copy.51
  140.7 45.9 %all_to_all.11 = bf16[64,6,1536]{2,1,0:T(8,128)(2,1)S(1)} all-to-all(bf16[64,6,1536]{2,1,0:T(8,128)(2,1)S(1)} %copy.51), channel_id=1, replica_groups=mesh['rep'=2,'req'=32,'tp'=4] {'rep','req'}, dimensions={0} | all-to-all | bytes 2359296 | tf_op jit(solution)/shard_map/all_to_all | solution.py:190
  186.6 1.2 reshape.206
  187.8 1.8 convolution_convert_fusion.2
  189.6 0.9 copy.54
  190.6 19.2 %reduce-scatter.4.cloned.1.call-done = bf16[384,16]{1,0:T(8,128)(2,1)} async-done(((bf16[1536,16]{1,0:T(8,128)(2,1)}), bf16[384,16]{1,0:T(8,128)(2,1)}) %reduce-scatter.4.cloned.1.call-update) | async-done | bytes 12304
  209.7 1.0 copy.55
  210.7 0.6 add_convert_fusion.1
  (66 shorter events, 2.8 us)
Async XLA Ops:
  6.5 57.9 %copy-start = (bf16[384,1536]{1,0:T(8,128)(2,1)S(1)}, bf16[384,1536]{1,0:T(8,128)(2,1)}, u32[]{:S(2)}) copy-start(bf16[384,1536]{1,0:T(8,128)(2,1)} %param.21) | copy-start | bytes 3538948
  6.5 203.2 %reduce-scatter.4.cloned.1.call-start = ((), (), s32[]{:S(2)}) async-start(), calls=%async_computation.3 | async-start | bytes 491520
  14.8 22.5 %collective-permute-start = (bf16[1,262528]{1,0:T(2,128)(2,1)}, bf16[1,262528]{1,0:T(2,128)(2,1)S(1)}, u32[]{:S(2)}, u32[]{:S(2)}) collective-permute-start(bf16[1,262528]{1,0:T(2,128)(2,1)} %pad_maximum_fusion), channel_id=1, source_target_pairs={{0,128},{128,0},{1,129},{129,1},{2,130},{130,2},{3,131},{131,3},{4... | collective-permute-start | bytes 1575176 | tf_op jit(solution)/shard_map/ppermute | solution.py:31
  14.8 21.2 %copy-start.6 = (s32[16,8]{0,1:T(8,128)S(1)}, s32[16,8]{0,1:T(8,128)}, u32[]{:S(2)}) copy-start(s32[16,8]{0,1:T(8,128)} %param.24) | copy-start | bytes 1540
  14.8 21.9 %copy-start.7 = (f32[16,8]{0,1:T(8,128)S(1)}, f32[16,8]{0,1:T(8,128)}, u32[]{:S(2)}) copy-start(f32[16,8]{0,1:T(8,128)} %param.25) | copy-start | bytes 1540
  14.8 22.2 %copy-start.8 = (s32[2,16]{1,0:T(2,128)S(1)}, s32[2,16]{1,0:T(2,128)}, u32[]{:S(2)}) copy-start(s32[2,16]{1,0:T(2,128)} %param.14) | copy-start | bytes 388
  37.3 13.4 %collective-permute-start.1 = (bf16[16,384]{1,0:T(8,128)(2,1)S(1)}, bf16[16,384]{1,0:T(8,128)(2,1)S(1)}, u32[]{:S(2)}, u32[]{:S(2)}) collective-permute-start(bf16[16,384]{1,0:T(8,128)(2,1)S(1)} %dynamic_update_slice.18), channel_id=1, source_target_pairs={{0,1},{1,2},{2,3},{3,0},{4,5},{5,6},{6,7},{7,4},{8,9},{9,10},{10,1... | collective-permute-start | bytes 36872 | tf_op jit(solution)/shard_map/ppermute | solution.py:20
  38.9 12.4 %collective-permute-start.2 = (bf16[16,384]{1,0:T(8,128)(2,1)S(1)}, bf16[16,384]{1,0:T(8,128)(2,1)S(1)}, u32[]{:S(2)}, u32[]{:S(2)}) collective-permute-start(bf16[16,384]{1,0:T(8,128)(2,1)S(1)} %dynamic_update_slice.18), channel_id=1, source_target_pairs={{0,3},{1,0},{2,1},{3,2},{4,7},{5,4},{6,5},{7,6},{8,11},{9,8},{10,9... | collective-permute-start | bytes 36872 | tf_op jit(solution)/shard_map/ppermute | solution.py:23
  49.4 6.7 %copy-start.1 = (bf16[1536,384]{1,0:T(8,128)(2,1)S(1)}, bf16[1536,384]{1,0:T(8,128)(2,1)}, u32[]{:S(2)}) copy-start(bf16[1536,384]{1,0:T(8,128)(2,1)} %param.19) | copy-start | bytes 3538948
  49.4 6.6 %copy-start.4 = (f32[1536]{0:T(1024)S(1)}, f32[1536]{0:T(1024)}, u32[]{:S(2)}) copy-start(f32[1536]{0:T(1024)} %param.17) | copy-start | bytes 18436
  50.7 5.8 %copy-start.2 = (bf16[1536,256]{1,0:T(8,128)(2,1)S(1)}, bf16[1536,256]{1,0:T(8,128)(2,1)}, u32[]{:S(2)}) copy-start(bf16[1536,256]{1,0:T(8,128)(2,1)} %param.20) | copy-start | bytes 2359300
  50.8 5.2 %collective-permute-start.3 = (bf16[16,384]{1,0:T(8,128)(2,1)S(1)}, bf16[16,384]{1,0:T(8,128)(2,1)S(1)}, u32[]{:S(2)}, u32[]{:S(2)}) collective-permute-start(bf16[16,384]{1,0:T(8,128)(2,1)S(1)} %collective-permute-done.1), channel_id=1, source_target_pairs={{0,1},{1,2},{2,3},{3,0},{4,5},{5,6},{6,7},{7,4},{8,9},{9,10},{10,1... | collective-permute-start | bytes 36872 | tf_op jit(solution)/shard_map/ppermute | solution.py:20
  64.3 15.5 %copy-start.5 = (f32[1536]{0:T(1024)S(1)}, f32[1536]{0:T(1024)}, u32[]{:S(2)}) copy-start(f32[1536]{0:T(1024)} %param.18) | copy-start | bytes 18436
  137.7 1.8 copy-start.3
Sparse Core Ops, SparseCore 0:
  190.7 18.9 reduce-scatter.3
